TPU v7x, 32 devices: a whole 2x2x4 slice. The times are simulated.
32 devices in a mesh: frame: 4 (over y, x), row: 8 (over z, core).
Axes of the slice: x: 2, y: 2, z: 4, core: 2. Of those that a mesh axis runs over, the one named last changes fastest.
Arguments:
- frames_in: bfloat16 [8, 32, 32, 256], P('frame', 'row'), may hold values from -6 to 6
- conv_first: bfloat16 [3, 3, 256, 256], replicated, may hold values from -0.125 to 0.125
- conv_second: bfloat16 [3, 3, 256, 256], replicated, may hold values from -0.125 to 0.125
- time_kernel: bfloat16 [3, 256, 256], replicated, may hold values from -0.21875 to 0.21875
- norm_gain: float32 [256], replicated, may hold values from 0.1 to 1.9
- w_query: bfloat16 [256, 256], replicated, may hold values from -0.375 to 0.375
- w_key: bfloat16 [256, 256], replicated, may hold values from -0.375 to 0.375
- w_value: bfloat16 [256, 256], replicated, may hold values from -0.375 to 0.375
- w_out: bfloat16 [256, 256], replicated, may hold values from -0.375 to 0.375
- frame_bias: float32 [8, 8], replicated, may hold values from -6 to 400
- conv_third: bfloat16 [3, 3, 256, 256], replicated, may hold values from -0.125 to 0.125
Outputs:
- encoded: bfloat16 [8, 32, 32, 256], P(None, 'row', 'frame')
All inputs are finite; a program needn't handle non-finite values.
Results may differ from a plain program's by a relative error of at most 0.018.
Values may be sent and summed in bfloat16 or wider, within the bound.
A program may use at most 64 MiB of HBM per device.

v0:
```python
import math

import jax
import jax.numpy as jnp
from jax import lax
from jax.sharding import PartitionSpec as P


def extended(cells, sides, width):
    for axis, dim in sides:
        count = lax.axis_size(axis)
        ends = count - 1
        head = lax.slice_in_dim(cells, 0, width, axis=dim)
        tail = lax.slice_in_dim(cells, cells.shape[dim] - width, cells.shape[dim], axis=dim)
        cells = jnp.concatenate(
            [
                lax.ppermute(tail, axis, [(i, (i + 1) % count) for i in range(ends)]),
                cells,
                lax.ppermute(head, axis, [((i + 1) % count, i) for i in range(ends)]),
            ],
            axis=dim,
        )
    return cells


def spatial(padded, weight, row_count, col_count):
    channels = weight.shape[2]
    summed = jnp.zeros((padded.shape[0] * row_count * col_count, weight.shape[3]), jnp.float32)
    for row_tap in range(3):
        for col_tap in range(3):
            window = padded[:, row_tap : row_tap + row_count, col_tap : col_tap + col_count, :]
            summed = summed + jnp.dot(
                window.reshape(-1, channels),
                weight[row_tap, col_tap],
                preferred_element_type=jnp.float32,
            )
    return summed.reshape(padded.shape[0], row_count, col_count, weight.shape[3])


def pad_columns(field):
    return jnp.pad(field, ((0, 0), (0, 0), (1, 1), (0, 0)))


def temporal(moved, time_kernel, norm_gain, w_query, w_key, w_value, w_out, frame_bias):
    frame_count = moved.shape[0]
    channels = moved.shape[-1]
    pixels = moved.reshape(frame_count, -1, channels)
    padded = jnp.pad(pixels, ((1, 1), (0, 0), (0, 0)))
    summed = pixels.astype(jnp.float32)
    for tap in range(3):
        shifted = padded[tap : tap + frame_count].reshape(-1, channels)
        summed = summed + jnp.dot(
            shifted, time_kernel[tap], preferred_element_type=jnp.float32
        ).reshape(pixels.shape)
    timed = summed.astype(jnp.bfloat16)
    widened = timed.astype(jnp.float32)
    scale_inv = lax.rsqrt(jnp.mean(widened * widened, axis=-1, keepdims=True) + 1e-06)
    normed = (widened * scale_inv * norm_gain).astype(jnp.bfloat16).reshape(-1, channels)
    queries = (
        jnp.dot(normed, w_query, preferred_element_type=jnp.float32)
        .astype(jnp.bfloat16)
        .reshape(pixels.shape)
    )
    key_rows = (
        jnp.dot(normed, w_key, preferred_element_type=jnp.float32)
        .astype(jnp.bfloat16)
        .reshape(pixels.shape)
    )
    value_rows = (
        jnp.dot(normed, w_value, preferred_element_type=jnp.float32)
        .astype(jnp.bfloat16)
        .reshape(pixels.shape)
    )
    scores = jnp.einsum(
        "fpc,gpc->pfg", queries, key_rows, preferred_element_type=jnp.float32
    ) / math.sqrt(channels)
    scores = scores + frame_bias
    peak = jnp.max(scores, axis=-1, keepdims=True)
    raised = jnp.exp(scores - peak)
    probs = (raised / jnp.sum(raised, axis=-1, keepdims=True)).astype(jnp.bfloat16)
    context = jnp.einsum(
        "pfg,gpc->fpc", probs, value_rows, preferred_element_type=jnp.float32
    ).astype(jnp.bfloat16)
    projected = jnp.dot(
        context.reshape(-1, channels), w_out, preferred_element_type=jnp.float32
    ).reshape(pixels.shape)
    return (widened + projected).astype(jnp.bfloat16).reshape(moved.shape)


def on_device(
    frames_in,
    conv_first,
    conv_second,
    time_kernel,
    norm_gain,
    w_query,
    w_key,
    w_value,
    w_out,
    frame_bias,
    conv_third,
):
    row_count = frames_in.shape[1]
    col_whole = frames_in.shape[2]
    haloed = extended(frames_in, (("row", 1),), 1)
    first = jax.nn.silu(spatial(pad_columns(haloed), conv_first, row_count, col_whole)).astype(
        jnp.bfloat16
    )
    haloed_two = extended(first, (("row", 1),), 1)
    second = jax.nn.silu(
        spatial(pad_columns(haloed_two), conv_second, row_count, col_whole)
    ).astype(jnp.bfloat16)
    moved = lax.all_to_all(second, "frame", split_axis=2, concat_axis=0, tiled=True)
    attended = temporal(moved, time_kernel, norm_gain, w_query, w_key, w_value, w_out, frame_bias)
    col_count = attended.shape[2]
    framed_last = extended(attended, (("frame", 2), ("row", 1)), 1)
    return spatial(framed_last, conv_third, row_count, col_count).astype(jnp.bfloat16)


def solution(mesh):
    placed = (P("frame", "row", None, None), P(), P(), P(), P(), P(), P(), P(), P(), P(), P())
    return jax.shard_map(
        on_device,
        mesh=mesh,
        in_specs=placed,
        out_specs=P(None, "row", "frame", None),
        check_vma=False,
    )
```

profile of v0, /device:TPU:21, one launch (start us, length us, event | category | flops | bytes accessed | tf_op | source)
XLA Modules:
  0.0 54.3 jit_solution(5470945481003135327)
XLA Ops:
  0.0 0.9 %fusion.102 = (bf16[2,1,32,256]{3,2,1,0:T(8,128)(2,1)S(1)}, bf16[2,1,32,256]{3,2,1,0:T(8,128)(2,1)S(1)}) fusion(bf16[2,4,32,256]{3,2,1,0:T(8,128)(2,1)} %param.11), kind=kLoop, calls=%fused_computation.152 | loop fusion | bytes 131072 | tf_op jit(solution)/shard_map/slice | solution.py:14
  0.9 2.6 %collective-permute-start.1 = (bf16[2,1,32,256]{3,2,1,0:T(8,128)(2,1)S(1)}, bf16[2,1,32,256]{3,2,1,0:T(8,128)(2,1)S(1)}, u32[]{:S(2)}, u32[]{:S(2)}) collective-permute-start(bf16[2,1,32,256]{3,2,1,0:T(8,128)(2,1)S(1)} %get-tuple-element.38), channel_id=1, source_target_pairs={{1,0},{2,1},{3,2},{4,3},{5,4},{6,5},{7,6},{9,8},{10,9},{11,10},{12... | collective-permute-start | bytes 98312 | tf_op jit(solution)/shard_map/ppermute | solution.py:19
  3.5 3.1 %collective-permute-start = (bf16[2,1,32,256]{3,2,1,0:T(8,128)(2,1)S(1)}, bf16[2,1,32,256]{3,2,1,0:T(8,128)(2,1)S(1)}, u32[]{:S(2)}, u32[]{:S(2)}) collective-permute-start(bf16[2,1,32,256]{3,2,1,0:T(8,128)(2,1)S(1)} %get-tuple-element.37), channel_id=1, source_target_pairs={{0,1},{1,2},{2,3},{3,4},{4,5},{5,6},{6,7},{8,9},{9,10},{10,11},{11... | collective-permute-start | bytes 98312 | tf_op jit(solution)/shard_map/ppermute | solution.py:17
  6.6 1.0 %collective-permute-done = bf16[2,1,32,256]{3,2,1,0:T(8,128)(2,1)S(1)} collective-permute-done((bf16[2,1,32,256]{3,2,1,0:T(8,128)(2,1)S(1)}, bf16[2,1,32,256]{3,2,1,0:T(8,128)(2,1)S(1)}, u32[]{:S(2)}, u32[]{:S(2)}) %collective-permute-start) | collective-permute-done | bytes 32800 | tf_op jit(solution)/shard_map/ppermute | solution.py:17
  7.6 1.0 %fusion.19 = bf16[2,6,34,256]{3,2,1,0:T(8,128)(2,1)S(1)} fusion(bf16[2,1,32,256]{3,2,1,0:T(8,128)(2,1)S(1)} %collective-permute-done.1, bf16[2,4,32,256]{3,2,1,0:T(8,128)(2,1)} %param.11, bf16[2,1,32,256]{3,2,1,0:T(8,128)(2,1)S(1)} %collective-permute-done), kind=kLoop, calls=%fused_computation.58 | loop fusion | flops 1253376 | bytes 405504 | tf_op jit(solution)/shard_map/concatenate | solution.py:15
  9.1 0.4 copy-done.1
  11.0 3.2 %collective-permute-start.3 = (bf16[2,1,32,256]{3,2,1,0:T(8,128)(2,1)S(1)}, bf16[2,1,32,256]{3,2,1,0:T(8,128)(2,1)S(1)}, u32[]{:S(2)}, u32[]{:S(2)}) collective-permute-start(bf16[2,1,32,256]{3,2,1,0:T(8,128)(2,1)S(1)} %get-tuple-element.34), channel_id=1, source_target_pairs={{1,0},{2,1},{3,2},{4,3},{5,4},{6,5},{7,6},{9,8},{10,9},{11,10},{12... | collective-permute-start | bytes 98312 | tf_op jit(solution)/shard_map/ppermute | solution.py:19
  14.2 3.1 %collective-permute-start.2 = (bf16[2,1,32,256]{3,2,1,0:T(8,128)(2,1)S(1)}, bf16[2,1,32,256]{3,2,1,0:T(8,128)(2,1)S(1)}, u32[]{:S(2)}, u32[]{:S(2)}) collective-permute-start(bf16[2,1,32,256]{3,2,1,0:T(8,128)(2,1)S(1)} %get-tuple-element.33), channel_id=1, source_target_pairs={{0,1},{1,2},{2,3},{3,4},{4,5},{5,6},{6,7},{8,9},{9,10},{10,11},{11... | collective-permute-start | bytes 98312 | tf_op jit(solution)/shard_map/ppermute | solution.py:17
  17.3 1.0 %collective-permute-done.2 = bf16[2,1,32,256]{3,2,1,0:T(8,128)(2,1)S(1)} collective-permute-done((bf16[2,1,32,256]{3,2,1,0:T(8,128)(2,1)S(1)}, bf16[2,1,32,256]{3,2,1,0:T(8,128)(2,1)S(1)}, u32[]{:S(2)}, u32[]{:S(2)}) %collective-permute-start.2) | collective-permute-done | bytes 32800 | tf_op jit(solution)/shard_map/ppermute | solution.py:17
  19.5 0.2 convolution_add_fusion.12
  20.4 0.8 %copy.24 = bf16[2,4,32,256]{3,1,0,2:T(4,128)(2,1)} copy(bf16[2,4,32,256]{3,2,1,0:T(8,128)(2,1)S(1)} %multiply_convert_fusion.1) | data formatting | bytes 262144 | tf_op jit(solution)/shard_map/convert_element_type | solution.py:112
  21.1 3.7 %all-to-all-start = ((bf16[2,4,32,256]{3,1,0,2:T(4,128)(2,1)}), bf16[2,4,32,256]{3,1,0,2:T(4,128)(2,1)S(1)}, u32[]{:S(2)}, u32[]{:S(2)}) async-start(bf16[2,4,32,256]{3,1,0,2:T(4,128)(2,1)} %copy.24), calls=%async_computation | async-start | bytes 262144 | tf_op jit(solution)/shard_map/all_to_all | solution.py:113
  24.9 3.3 %all-to-all-done = bf16[2,4,32,256]{3,1,0,2:T(4,128)(2,1)S(1)} async-done(((bf16[2,4,32,256]{3,1,0,2:T(4,128)(2,1)}), bf16[2,4,32,256]{3,1,0,2:T(4,128)(2,1)S(1)}, u32[]{:S(2)}, u32[]{:S(2)}) %all-to-all-start) | async-done | bytes 131104 | tf_op jit(solution)/shard_map/all_to_all | solution.py:113
  28.6 0.3 multiply_reduce_fusion
  29.7 0.3 fusion.13
  30.0 0.3 fusion.11
  30.6 2.8 %collective-permute-start.5 = (bf16[8,4,1,256]{3,2,1,0:T(2,128)(2,1)S(1)}, bf16[8,4,1,256]{3,2,1,0:T(2,128)(2,1)S(1)}, u32[]{:S(2)}, u32[]{:S(2)}) collective-permute-start(bf16[8,4,1,256]{3,2,1,0:T(2,128)(2,1)S(1)} %get-tuple-element.30), channel_id=1, source_target_pairs={{8,0},{16,8},{24,16},{9,1},{17,9},{25,17},{10,2},{18,10},{26,18},{... | collective-permute-start | bytes 49160 | tf_op jit(solution)/shard_map/ppermute | solution.py:19
  33.4 2.5 %collective-permute-start.4 = (bf16[8,4,1,256]{3,2,1,0:T(2,128)(2,1)S(1)}, bf16[8,4,1,256]{3,2,1,0:T(2,128)(2,1)S(1)}, u32[]{:S(2)}, u32[]{:S(2)}) collective-permute-start(bf16[8,4,1,256]{3,2,1,0:T(2,128)(2,1)S(1)} %get-tuple-element.29), channel_id=1, source_target_pairs={{0,8},{8,16},{16,24},{1,9},{9,17},{17,25},{2,10},{10,18},{18,26},{... | collective-permute-start | bytes 49160 | tf_op jit(solution)/shard_map/ppermute | solution.py:17
  36.1 2.9 %collective-permute-done.4 = bf16[8,4,1,256]{3,2,1,0:T(2,128)(2,1)S(1)} collective-permute-done((bf16[8,4,1,256]{3,2,1,0:T(2,128)(2,1)S(1)}, bf16[8,4,1,256]{3,2,1,0:T(2,128)(2,1)S(1)}, u32[]{:S(2)}, u32[]{:S(2)}) %collective-permute-start.4) | collective-permute-done | bytes 16416 | tf_op jit(solution)/shard_map/ppermute | solution.py:17
  39.0 7.1 %collective-permute-start.6 = (bf16[8,1,10,256]{3,2,1,0:T(8,128)(2,1)S(1)}, bf16[8,1,10,256]{3,2,1,0:T(8,128)(2,1)S(1)}, u32[]{:S(2)}, u32[]{:S(2)}) collective-permute-start(bf16[8,1,10,256]{3,2,1,0:T(8,128)(2,1)S(1)} %get-tuple-element.25), channel_id=1, source_target_pairs={{0,1},{1,2},{2,3},{3,4},{4,5},{5,6},{6,7},{8,9},{9,10},{10,11},{11... | collective-permute-start | bytes 122888 | tf_op jit(solution)/shard_map/ppermute | solution.py:17
  46.1 1.9 %collective-permute-start.7 = (bf16[8,1,10,256]{3,2,1,0:T(8,128)(2,1)S(1)}, bf16[8,1,10,256]{3,2,1,0:T(8,128)(2,1)S(1)}, u32[]{:S(2)}, u32[]{:S(2)}) collective-permute-start(bf16[8,1,10,256]{3,2,1,0:T(8,128)(2,1)S(1)} %get-tuple-element.26), channel_id=1, source_target_pairs={{1,0},{2,1},{3,2},{4,3},{5,4},{6,5},{7,6},{9,8},{10,9},{11,10},{12... | collective-permute-start | bytes 122888 | tf_op jit(solution)/shard_map/ppermute | solution.py:19
  48.2 3.5 %collective-permute-done.7 = bf16[8,1,10,256]{3,2,1,0:T(8,128)(2,1)S(1)} collective-permute-done((bf16[8,1,10,256]{3,2,1,0:T(8,128)(2,1)S(1)}, bf16[8,1,10,256]{3,2,1,0:T(8,128)(2,1)S(1)}, u32[]{:S(2)}, u32[]{:S(2)}) %collective-permute-start.7) | collective-permute-done | bytes 40992 | tf_op jit(solution)/shard_map/ppermute | solution.py:19
  51.7 0.3 maximum_maximum_fusion
  53.5 0.8 %fusion.7 = bf16[256,256]{1,0:T(8,128)(2,1)} fusion(f32[256,256]{1,0:T(8,128)S(1)} %convolution_add_fusion.3, bf16[256,256]{1,0:T(8,128)(2,1)S(1)} %bitcast.189, bf16[3,3,256,256]{3,2,1,0:T(8,128)(2,1)S(1)} %copy-done.3), kind=kOutput, calls=%fused_computation.30 | convolution fusion | flops 33685504 | bytes 655360 | tf_op jit(solution)/shard_map/dot_general | solution.py:32
  (73 shorter events, 7.1 us)
Async XLA Ops:
  0.0 29.0 %copy-start = (bf16[256,256]{1,0:T(8,128)(2,1)S(1)}, bf16[256,256]{1,0:T(8,128)(2,1)}, u32[]{:S(2)}) copy-start(bf16[256,256]{1,0:T(8,128)(2,1)} %param.18) | copy-start | bytes 393220
  0.0 8.7 %copy-start.2 = (bf16[3,3,256,256]{3,2,1,0:T(8,128)(2,1)S(1)}, bf16[3,3,256,256]{3,2,1,0:T(8,128)(2,1)}, u32[]{:S(2)}) copy-start(bf16[3,3,256,256]{3,2,1,0:T(8,128)(2,1)} %param.12) | copy-start | bytes 3538948
  0.9 5.7 %collective-permute-start.1 = (bf16[2,1,32,256]{3,2,1,0:T(8,128)(2,1)S(1)}, bf16[2,1,32,256]{3,2,1,0:T(8,128)(2,1)S(1)}, u32[]{:S(2)}, u32[]{:S(2)}) collective-permute-start(bf16[2,1,32,256]{3,2,1,0:T(8,128)(2,1)S(1)} %get-tuple-element.38), channel_id=1, source_target_pairs={{1,0},{2,1},{3,2},{4,3},{5,4},{6,5},{7,6},{9,8},{10,9},{11,10},{12... | collective-permute-start | bytes 98312 | tf_op jit(solution)/shard_map/ppermute | solution.py:19
  3.5 4.1 %collective-permute-start = (bf16[2,1,32,256]{3,2,1,0:T(8,128)(2,1)S(1)}, bf16[2,1,32,256]{3,2,1,0:T(8,128)(2,1)S(1)}, u32[]{:S(2)}, u32[]{:S(2)}) collective-permute-start(bf16[2,1,32,256]{3,2,1,0:T(8,128)(2,1)S(1)} %get-tuple-element.37), channel_id=1, source_target_pairs={{0,1},{1,2},{2,3},{3,4},{4,5},{5,6},{6,7},{8,9},{9,10},{10,11},{11... | collective-permute-start | bytes 98312 | tf_op jit(solution)/shard_map/ppermute | solution.py:17
  8.6 0.9 %copy-start.1 = (bf16[2,4,32,256]{3,2,1,0:T(8,128)(2,1)S(1)}, bf16[2,4,32,256]{3,2,1,0:T(8,128)(2,1)}, u32[]{:S(2)}) copy-start(bf16[2,4,32,256]{3,2,1,0:T(8,128)(2,1)} %param.11) | copy-start | bytes 393220
  10.9 7.6 %copy-start.4 = (bf16[3,3,256,256]{3,2,1,0:T(8,128)(2,1)S(1)}, bf16[3,3,256,256]{3,2,1,0:T(8,128)(2,1)}, u32[]{:S(2)}) copy-start(bf16[3,3,256,256]{3,2,1,0:T(8,128)(2,1)} %param.13) | copy-start | bytes 3538948
  11.0 6.3 %collective-permute-start.3 = (bf16[2,1,32,256]{3,2,1,0:T(8,128)(2,1)S(1)}, bf16[2,1,32,256]{3,2,1,0:T(8,128)(2,1)S(1)}, u32[]{:S(2)}, u32[]{:S(2)}) collective-permute-start(bf16[2,1,32,256]{3,2,1,0:T(8,128)(2,1)S(1)} %get-tuple-element.34), channel_id=1, source_target_pairs={{1,0},{2,1},{3,2},{4,3},{5,4},{6,5},{7,6},{9,8},{10,9},{11,10},{12... | collective-permute-start | bytes 98312 | tf_op jit(solution)/shard_map/ppermute | solution.py:19
  14.2 4.1 %collective-permute-start.2 = (bf16[2,1,32,256]{3,2,1,0:T(8,128)(2,1)S(1)}, bf16[2,1,32,256]{3,2,1,0:T(8,128)(2,1)S(1)}, u32[]{:S(2)}, u32[]{:S(2)}) collective-permute-start(bf16[2,1,32,256]{3,2,1,0:T(8,128)(2,1)S(1)} %get-tuple-element.33), channel_id=1, source_target_pairs={{0,1},{1,2},{2,3},{3,4},{4,5},{5,6},{6,7},{8,9},{9,10},{10,11},{11... | collective-permute-start | bytes 98312 | tf_op jit(solution)/shard_map/ppermute | solution.py:17
  20.1 4.7 %copy-start.9 = (f32[8,8]{1,0:T(8,128)S(1)}, f32[8,8]{1,0:T(8,128)}, u32[]{:S(2)}) copy-start(f32[8,8]{1,0:T(8,128)} %param.20) | copy-start | bytes 772
  20.1 8.1 %copy-start.5 = (bf16[3,256,256]{2,1,0:T(8,128)(2,1)S(1)}, bf16[3,256,256]{2,1,0:T(8,128)(2,1)}, u32[]{:S(2)}) copy-start(bf16[3,256,256]{2,1,0:T(8,128)(2,1)} %param.14) | copy-start | bytes 1179652
  21.1 7.0 %all-to-all-start = ((bf16[2,4,32,256]{3,1,0,2:T(4,128)(2,1)}), bf16[2,4,32,256]{3,1,0,2:T(4,128)(2,1)S(1)}, u32[]{:S(2)}, u32[]{:S(2)}) async-start(bf16[2,4,32,256]{3,1,0,2:T(4,128)(2,1)} %copy.24), calls=%async_computation | async-start | bytes 262144 | tf_op jit(solution)/shard_map/all_to_all | solution.py:113
  28.1 0.7 %copy-start.10 = (f32[256]{0:T(256)S(1)}, f32[256]{0:T(256)}, u32[]{:S(2)}) copy-start(f32[256]{0:T(256)} %param.15) | copy-start | bytes 3076
  28.4 0.9 %copy-start.6 = (bf16[256,256]{1,0:T(8,128)(2,1)S(1)}, bf16[256,256]{1,0:T(8,128)(2,1)}, u32[]{:S(2)}) copy-start(bf16[256,256]{1,0:T(8,128)(2,1)} %param.17) | copy-start | bytes 393220
  28.6 0.9 %copy-start.7 = (bf16[256,256]{1,0:T(8,128)(2,1)S(1)}, bf16[256,256]{1,0:T(8,128)(2,1)}, u32[]{:S(2)}) copy-start(bf16[256,256]{1,0:T(8,128)(2,1)} %param.16) | copy-start | bytes 393220
  29.3 1.0 %copy-start.8 = (bf16[256,256]{1,0:T(8,128)(2,1)S(1)}, bf16[256,256]{1,0:T(8,128)(2,1)}, u32[]{:S(2)}) copy-start(bf16[256,256]{1,0:T(8,128)(2,1)} %param.19) | copy-start | bytes 393220
  29.7 6.2 %copy-start.3 = (bf16[3,3,256,256]{3,2,1,0:T(8,128)(2,1)S(1)}, bf16[3,3,256,256]{3,2,1,0:T(8,128)(2,1)}, u32[]{:S(2)}) copy-start(bf16[3,3,256,256]{3,2,1,0:T(8,128)(2,1)} %param.21) | copy-start | bytes 3538948
  30.6 5.5 %collective-permute-start.5 = (bf16[8,4,1,256]{3,2,1,0:T(2,128)(2,1)S(1)}, bf16[8,4,1,256]{3,2,1,0:T(2,128)(2,1)S(1)}, u32[]{:S(2)}, u32[]{:S(2)}) collective-permute-start(bf16[8,4,1,256]{3,2,1,0:T(2,128)(2,1)S(1)} %get-tuple-element.30), channel_id=1, source_target_pairs={{8,0},{16,8},{24,16},{9,1},{17,9},{25,17},{10,2},{18,10},{26,18},{... | collective-permute-start | bytes 49160 | tf_op jit(solution)/shard_map/ppermute | solution.py:19
  33.4 5.6 %collective-permute-start.4 = (bf16[8,4,1,256]{3,2,1,0:T(2,128)(2,1)S(1)}, bf16[8,4,1,256]{3,2,1,0:T(2,128)(2,1)S(1)}, u32[]{:S(2)}, u32[]{:S(2)}) collective-permute-start(bf16[8,4,1,256]{3,2,1,0:T(2,128)(2,1)S(1)} %get-tuple-element.29), channel_id=1, source_target_pairs={{0,8},{8,16},{16,24},{1,9},{9,17},{17,25},{2,10},{10,18},{18,26},{... | collective-permute-start | bytes 49160 | tf_op jit(solution)/shard_map/ppermute | solution.py:17
  39.0 9.2 %collective-permute-start.6 = (bf16[8,1,10,256]{3,2,1,0:T(8,128)(2,1)S(1)}, bf16[8,1,10,256]{3,2,1,0:T(8,128)(2,1)S(1)}, u32[]{:S(2)}, u32[]{:S(2)}) collective-permute-start(bf16[8,1,10,256]{3,2,1,0:T(8,128)(2,1)S(1)} %get-tuple-element.25), channel_id=1, source_target_pairs={{0,1},{1,2},{2,3},{3,4},{4,5},{5,6},{6,7},{8,9},{9,10},{10,11},{11... | collective-permute-start | bytes 122888 | tf_op jit(solution)/shard_map/ppermute | solution.py:17
  46.1 5.6 %collective-permute-start.7 = (bf16[8,1,10,256]{3,2,1,0:T(8,128)(2,1)S(1)}, bf16[8,1,10,256]{3,2,1,0:T(8,128)(2,1)S(1)}, u32[]{:S(2)}, u32[]{:S(2)}) collective-permute-start(bf16[8,1,10,256]{3,2,1,0:T(8,128)(2,1)S(1)} %get-tuple-element.26), channel_id=1, source_target_pairs={{1,0},{2,1},{3,2},{4,3},{5,4},{6,5},{7,6},{9,8},{10,9},{11,10},{12... | collective-permute-start | bytes 122888 | tf_op jit(solution)/shard_map/ppermute | solution.py:19
where the time goes:
time: 54.8 us; the launch traced here: 54.3 us
  starting transfers between devices  29.9 us (55%)
  waiting for transfers between devices  11.6 us (21%)
  matrix products  7.61 us (14%)
  local copies, waits for them, and re-layouts  2.71 us (5%)
  other arithmetic  1.94 us (4%)
  between operations  0.57 us (1%)
    ppermute x4, starting transfers between devices, extended(): lax.ppermute(tail, axis, [(i, (i + 1) % count) for i in range(ends)])  15.8 us
    ppermute x4, starting transfers between devices, extended(): lax.ppermute(head, axis, [((i + 1) % count, i) for i in range(ends)])  10.5 us
    dot_general x27, matrix products, spatial(): jnp.dot(window.reshape(-1, channels), weight[row_tap, col_tap], preferred...  5.71 us
    ppermute x4, waiting for transfers between devices, extended(): lax.ppermute(tail, axis, [(i, (i + 1) % count) for i in range(ends)])  4.84 us
    all_to_all x1, starting transfers between devices, on_device(): lax.all_to_all(second, 'frame', split_axis=2, concat_axis=0, tiled=True)  3.67 us
    ppermute x4, waiting for transfers between devices, extended(): lax.ppermute(head, axis, [((i + 1) % count, i) for i in range(ends)])  3.52 us
    all_to_all x1, waiting for transfers between devices, on_device(): lax.all_to_all(second, 'frame', split_axis=2, concat_axis=0, tiled=True)  3.27 us
    concatenate x6, other arithmetic, extended(): jnp.concatenate([lax.ppermute(tail, axis, [(i, (i + 1) % count) for i in...  1.53 us
  transfers between devices with their start and end apart: 9, of which 5 were waited for; matrix products, arithmetic and copies ran while one was open for 1% of the time, Pallas kernels for 0%

commit v1 on v0

v1 whole, which is shorter than its diff:
```python
import functools
import math

import jax
import jax.numpy as jnp
from jax import lax
from jax.experimental import pallas as pl
from jax.experimental.pallas import tpu as pltpu
from jax.sharding import PartitionSpec as P

MESH = pl.DeviceIdType.MESH
BF16 = jnp.bfloat16
F32 = jnp.float32
HALO = 3
GROUP = 16


def matmul(lhs, rhs):
    return jnp.dot(lhs, rhs, preferred_element_type=F32)


def silu(v):
    return 0.5 * v * (1.0 + jnp.tanh(0.5 * v))


def steps_below(index, pitch, count):
    quotient = jnp.zeros_like(index)
    for k in range(1, count):
        quotient = quotient + (index >= k * pitch).astype(jnp.int32)
    return quotient


def shifted_columns(rows, width):
    count, _, channels = rows.shape
    flat = rows.astype(F32).reshape(count * width, channels)
    column = lax.broadcasted_iota(jnp.int32, (count, width, channels), 1)
    left = pltpu.roll(flat, 1, 0).reshape(count, width, channels)
    right = pltpu.roll(flat, count * width - 1, 0).reshape(count, width, channels)
    left = jnp.where(column == 0, 0.0, left).astype(BF16)
    right = jnp.where(column == width - 1, 0.0, right).astype(BF16)
    return left, right


def kernel(
    frames_axis,
    rows_axis,
    x_hbm,
    w1_hbm,
    w2_hbm,
    tk_hbm,
    gain_ref,
    wq_hbm,
    wk_hbm,
    wv_hbm,
    wo_hbm,
    bias_ref,
    w3_hbm,
    out_ref,
    xin,
    xs,
    fs,
    w1,
    w2,
    tk,
    wq,
    wk,
    wv,
    wo,
    w3,
    pick,
    packed,
    moved,
    context,
    cols3,
    local_sem,
    halo_send,
    halo_recv,
    send_sem,
    recv_sem,
):
    frame = lax.axis_index("frame")
    row = lax.axis_index("row")
    local_frames, row_count, width, channels = x_hbm.shape
    frame_count = frames_axis * local_frames
    cols = width // frames_axis
    pitch = cols + 2
    tile_rows = row_count + 2
    slots = packed.shape[2]
    height = row_count * rows_axis

    own = pltpu.make_async_copy(x_hbm, xin.at[:, HALO : HALO + row_count], local_sem.at[0])
    own.start()
    loads = []
    for k, (src, dst) in enumerate(
        ((w1_hbm, w1), (w2_hbm, w2), (tk_hbm, tk), (wq_hbm, wq), (wk_hbm, wk), (wv_hbm, wv), (wo_hbm, wo), (w3_hbm, w3))
    ):
        load = pltpu.make_async_copy(src, dst, local_sem.at[k + 1])
        load.start()
        loads.append(load)

    barrier = pltpu.get_barrier_semaphore()
    above = lax.rem(row + rows_axis - 1, rows_axis)
    below = lax.rem(row + 1, rows_axis)

    @pl.when(row > 0)
    def _():
        pl.semaphore_signal(barrier, inc=1, device_id={"row": above}, device_id_type=MESH)

    @pl.when(row < rows_axis - 1)
    def _():
        pl.semaphore_signal(barrier, inc=1, device_id={"row": below}, device_id_type=MESH)

    for k in range(1, frames_axis):
        peer = lax.rem(frame + k, frames_axis)
        pl.semaphore_signal(barrier, inc=1, device_id={"frame": peer}, device_id_type=MESH)
    neighbours = (row > 0).astype(jnp.int32) + (row < rows_axis - 1).astype(jnp.int32)
    pl.semaphore_wait(barrier, neighbours + (frames_axis - 1))

    up = pltpu.make_async_remote_copy(
        src_ref=x_hbm.at[:, 0:HALO],
        dst_ref=xin.at[:, HALO + row_count : 2 * HALO + row_count],
        send_sem=halo_send.at[1],
        recv_sem=halo_recv.at[1],
        device_id={"row": above},
        device_id_type=MESH,
    )
    down = pltpu.make_async_remote_copy(
        src_ref=x_hbm.at[:, row_count - HALO : row_count],
        dst_ref=xin.at[:, 0:HALO],
        send_sem=halo_send.at[0],
        recv_sem=halo_recv.at[0],
        device_id={"row": below},
        device_id_type=MESH,
    )

    @pl.when(row > 0)
    def _():
        up.start()

    @pl.when(row < rows_axis - 1)
    def _():
        down.start()

    blank = jnp.zeros((local_frames, HALO, width, channels), BF16)

    @pl.when(row == 0)
    def _():
        xin[:, 0:HALO] = blank

    @pl.when(row == rows_axis - 1)
    def _():
        xin[:, HALO + row_count : 2 * HALO + row_count] = blank

    target = lax.broadcasted_iota(jnp.int32, (frames_axis * slots, tile_rows * width), 0)
    source = lax.broadcasted_iota(jnp.int32, (frames_axis * slots, tile_rows * width), 1)
    owner = steps_below(target, slots, frames_axis)
    slot = target - owner * slots
    slot_row = steps_below(slot, pitch, tile_rows)
    slot_col = slot - slot_row * pitch + owner * cols - 1
    wanted = slot_row * width + slot_col
    taken = (
        (slot < tile_rows * pitch) & (slot_col >= 0) & (slot_col < width) & (source == wanted)
    )
    pick[...] = jnp.where(taken, 1.0, 0.0).astype(BF16)
    edge = jnp.zeros((1, slots, channels), BF16)
    moved[0:1] = edge
    moved[frame_count + 1 : frame_count + 2] = edge

    def spread(first_row, last_row):
        for f in range(local_frames):
            rows = xin[f, first_row:last_row]
            left, right = shifted_columns(rows, width)
            xs[f, first_row:last_row, :, 0:channels] = left
            xs[f, first_row:last_row, :, channels : 2 * channels] = rows
            xs[f, first_row:last_row, :, 2 * channels : 3 * channels] = right

    own.wait()
    spread(HALO, HALO + row_count)
    loads[0].wait()

    @pl.when(row > 0)
    def _():
        down.wait_recv()

    @pl.when(row < rows_axis - 1)
    def _():
        up.wait_recv()

    spread(0, HALO)
    spread(HALO + row_count, 2 * HALO + row_count)

    first_rows = row_count + 4
    image_row = (
        lax.broadcasted_iota(jnp.int32, (first_rows, width, channels), 0) + row * row_count - 2
    )
    first_in = (image_row >= 0) & (image_row < height)
    image_row = (
        lax.broadcasted_iota(jnp.int32, (tile_rows, width, channels), 0) + row * row_count - 1
    )
    second_in = (image_row >= 0) & (image_row < height)
    for f in range(local_frames):
        summed = None
        for a in range(3):
            part = matmul(
                xs[f, a : a + first_rows].reshape(first_rows * width, 3 * channels),
                w1[a].reshape(3 * channels, channels),
            )
            summed = part if summed is None else summed + part
        first = silu(summed).reshape(first_rows, width, channels)
        first = jnp.where(first_in, first, 0.0).astype(BF16)
        left, right = shifted_columns(first, width)
        fs[f, :, :, 0:channels] = left
        fs[f, :, :, channels : 2 * channels] = first
        fs[f, :, :, 2 * channels : 3 * channels] = right

    loads[1].wait()
    exchanges = []
    for f in range(local_frames):
        summed = None
        for a in range(3):
            part = matmul(
                fs[f, a : a + tile_rows].reshape(tile_rows * width, 3 * channels),
                w2[a].reshape(3 * channels, channels),
            )
            summed = part if summed is None else summed + part
        second = silu(summed).reshape(tile_rows, width, channels)
        second = jnp.where(second_in, second, 0.0).astype(BF16).reshape(tile_rows * width, channels)
        packed[f] = matmul(pick[...], second).astype(BF16).reshape(frames_axis, slots, channels)
        for k in range(1, frames_axis):
            peer = lax.rem(frame + k, frames_axis)
            exchange = pltpu.make_async_remote_copy(
                src_ref=packed.at[f, peer],
                dst_ref=moved.at[1 + frame * local_frames + f],
                send_sem=send_sem.at[f, k],
                recv_sem=recv_sem.at[f, k],
                device_id={"frame": peer},
                device_id_type=MESH,
            )
            exchange.start()
            exchanges.append(exchange)
        moved[1 + frame * local_frames + f] = packed[f, frame]

    span = frame_count * GROUP
    lane = lax.broadcasted_iota(jnp.int32, (frame_count, span), 1)
    wide = jnp.zeros((frame_count, span), F32)
    for g in range(frame_count):
        inside = (lane >= g * GROUP) & (lane < (g + 1) * GROUP)
        wide = jnp.where(inside, bias_ref[:, g : g + 1], wide)
    wide = jnp.broadcast_to(wide[:, None, :], (frame_count, GROUP, span)).reshape(span, span)
    query_pixel = jnp.bitwise_and(lax.broadcasted_iota(jnp.int32, (span, span), 0), GROUP - 1)
    key_pixel = jnp.bitwise_and(lax.broadcasted_iota(jnp.int32, (span, span), 1), GROUP - 1)
    masked_bias = jnp.where(query_pixel == key_pixel, wide, -1e30)

    taps = tile_rows * cols
    target = lax.broadcasted_iota(jnp.int32, (3 * taps, slots), 0)
    source = lax.broadcasted_iota(jnp.int32, (3 * taps, slots), 1)
    shift = steps_below(target, taps, 3)
    inner = target - shift * taps
    inner_row = steps_below(inner, cols, tile_rows)
    wanted = inner_row * pitch + inner - inner_row * cols + shift
    pick3 = jnp.where(source == wanted, 1.0, 0.0).astype(BF16)

    for load in loads[2:]:
        load.wait()
    for exchange in exchanges:
        exchange.wait_recv()

    pixels = frame_count * slots
    centre = moved[1 : 1 + frame_count].reshape(pixels, channels)
    summed = centre.astype(F32)
    for tap in range(3):
        summed = summed + matmul(moved[tap : tap + frame_count].reshape(pixels, channels), tk[tap])
    timed = summed.astype(BF16)
    widened = timed.astype(F32)
    scale_inv = lax.rsqrt(jnp.mean(widened * widened, axis=-1, keepdims=True) + 1e-06)
    normed = (widened * scale_inv * gain_ref[...]).astype(BF16)
    tile = (frame_count, slots, channels)
    queries = matmul(normed, wq[...]).astype(BF16).reshape(tile)
    key_rows = matmul(normed, wk[...]).astype(BF16).reshape(tile)
    value_rows = matmul(normed, wv[...]).astype(BF16).reshape(tile)
    for g in range(slots // GROUP):
        part = slice(g * GROUP, (g + 1) * GROUP)
        scores = lax.dot_general(
            queries[:, part].reshape(span, channels),
            key_rows[:, part].reshape(span, channels),
            (((1,), (1,)), ((), ())),
            preferred_element_type=F32,
        )
        scores = scores * (1.0 / math.sqrt(channels)) + masked_bias
        raised = jnp.exp(scores - jnp.max(scores, axis=-1, keepdims=True))
        probs = (raised / jnp.sum(raised, axis=-1, keepdims=True)).astype(BF16)
        mixed = matmul(probs, value_rows[:, part].reshape(span, channels))
        context[:, part] = mixed.astype(BF16).reshape(frame_count, GROUP, channels)
    attended = widened + matmul(context[...].reshape(pixels, channels), wo[...])
    attended = attended.astype(BF16).reshape(tile)

    count = row_count * cols
    for f in range(frame_count):
        gathered = matmul(pick3, attended[f])
        for a in range(3):
            for b in range(3):
                start = b * taps + a * cols
                cols3[a, f, :, b * channels : (b + 1) * channels] = gathered[
                    start : start + count
                ].astype(BF16)
    summed = None
    for a in range(3):
        part = matmul(
            cols3[a].reshape(frame_count * count, 3 * channels),
            w3[a].reshape(3 * channels, channels),
        )
        summed = part if summed is None else summed + part
    out_ref[...] = summed.reshape(frame_count, row_count, cols, channels).astype(BF16)

    @pl.when(row > 0)
    def _():
        up.wait_send()

    @pl.when(row < rows_axis - 1)
    def _():
        down.wait_send()

    for exchange in exchanges:
        exchange.wait_send()


def on_device(frames_axis, rows_axis, *args):
    frames_in = args[0]
    norm_gain = args[4]
    local_frames, row_count, width, channels = frames_in.shape
    frame_count = local_frames * frames_axis
    cols = width // frames_axis
    slots = -(-(row_count + 2) * (cols + 2) // GROUP) * GROUP
    args = args[:4] + (norm_gain.reshape(1, channels),) + args[5:]
    any_space = pl.BlockSpec(memory_space=pl.ANY)
    vmem = pl.BlockSpec(memory_space=pltpu.VMEM)
    weight = pltpu.VMEM((3, 3, channels, channels), BF16)
    square = pltpu.VMEM((channels, channels), BF16)
    return pl.pallas_call(
        functools.partial(kernel, frames_axis, rows_axis),
        out_shape=jax.ShapeDtypeStruct((frame_count, row_count, cols, channels), BF16),
        in_specs=[any_space] * 4 + [vmem] + [any_space] * 4 + [vmem, any_space],
        out_specs=vmem,
        scratch_shapes=[
            pltpu.VMEM((local_frames, row_count + 2 * HALO, width, channels), BF16),
            pltpu.VMEM((local_frames, row_count + 2 * HALO, width, 3 * channels), BF16),
            pltpu.VMEM((local_frames, row_count + 4, width, 3 * channels), BF16),
            weight,
            weight,
            pltpu.VMEM((3, channels, channels), BF16),
            square,
            square,
            square,
            square,
            weight,
            pltpu.VMEM((frames_axis * slots, (row_count + 2) * width), BF16),
            pltpu.VMEM((local_frames, frames_axis, slots, channels), BF16),
            pltpu.VMEM((frame_count + 2, slots, channels), BF16),
            pltpu.VMEM((frame_count, slots, channels), BF16),
            pltpu.VMEM((3, frame_count, row_count * cols, 3 * channels), BF16),
            pltpu.SemaphoreType.DMA((9,)),
            pltpu.SemaphoreType.DMA((2,)),
            pltpu.SemaphoreType.DMA((2,)),
            pltpu.SemaphoreType.DMA((local_frames, frames_axis)),
            pltpu.SemaphoreType.DMA((local_frames, frames_axis)),
        ],
        compiler_params=pltpu.CompilerParams(
            collective_id=0, has_side_effects=True, vmem_limit_bytes=56 * 1024 * 1024
        ),
    )(*args)


def solution(mesh):
    placed = (P("frame", "row", None, None),) + (P(),) * 10
    return jax.shard_map(
        functools.partial(on_device, mesh.shape["frame"], mesh.shape["row"]),
        mesh=mesh,
        in_specs=placed,
        out_specs=P(None, "row", "frame", None),
        check_vma=False,
    )
```

time: 54.8 us -> 18.3 us (0.33)
  the two profiles are of different devices: /device:TPU:21 before, /device:TPU:9 now
where the time goes in v1:
time: 18.3 us; the launch traced here: 18.1 us
  Pallas kernels  16.5 us (90%)
  local copies, waits for them, and re-layouts  1.57 us (9%)
    pallas_call x1, Pallas kernels, on_device(): pl.pallas_call(functools.partial(kernel, frames_axis, rows_axis), out_sha...  16.5 us
    unnamed x1, local copies, waits for them, and re-layouts  1.57 us

profile of v1, /device:TPU:9, one launch (start us, length us, event | category | flops | bytes accessed | tf_op | source)
XLA Modules:
  0.0 18.1 jit_solution(4644500272988134463)
XLA Ops:
  0.0 16.5 %shard_map.109 = bf16[8,4,8,256]{3,2,1,0:T(8,128)(2,1)} custom-call(bf16[2,4,32,256]{3,2,1,0:T(8,128)(2,1)} %x_hbm.1, bf16[3,3,256,256]{3,2,1,0:T(8,128)(2,1)} %w1_hbm.1, bf16[3,3,256,256]{3,2,1,0:T(8,128)(2,1)} %w2_hbm.1, bf16[3,256,256]{2,1,0:T(8,128)(2,1)} %tk_hbm.1, f32[1,256]{1,0:T(1,128)} %bitcast.1, bf16[256,256]{1,0:T(8,128)(2,1)} %wq_hbm.1, ...), custom_call_target="tpu_custom_call" | custom-call | tf_op jit(solution)/shard_map/pallas_call | solution.py:339
  16.5 1.6 %copy.13 = bf16[8,4,8,256]{3,2,1,0:T(8,128)(2,1)} copy(bf16[8,4,8,256]{3,2,1,0:T(8,128)(2,1)} %shard_map.109) | data formatting | bytes 262144

commit v2 on v1

--- a/solution.py
+++ b/solution.py
@@ -48,12 +48,12 @@
     w1_hbm,
     w2_hbm,
     tk_hbm,
-    gain_ref,
+    gain_hbm,
     wq_hbm,
     wk_hbm,
     wv_hbm,
     wo_hbm,
-    bias_ref,
+    bias_hbm,
     w3_hbm,
     out_ref,
     xin,
@@ -67,6 +67,9 @@
     wv,
     wo,
     w3,
+    partial,
+    gain_ref,
+    bias_ref,
     pick,
     packed,
     moved,
@@ -88,58 +91,59 @@
     slots = packed.shape[2]
     height = row_count * rows_axis
 
+    barrier = pltpu.get_barrier_semaphore()
+    above = lax.rem(row + rows_axis - 1, rows_axis)
+    below = lax.rem(row + 1, rows_axis)
+
+    @pl.when(row > 0)
+    def _():
+        pl.semaphore_signal(barrier, inc=1, device_id={"row": above}, device_id_type=MESH)
+
+    @pl.when(row < rows_axis - 1)
+    def _():
+        pl.semaphore_signal(barrier, inc=1, device_id={"row": below}, device_id_type=MESH)
+
+    for k in range(1, frames_axis):
+        peer = lax.rem(frame + k, frames_axis)
+        pl.semaphore_signal(barrier, inc=1, device_id={"frame": peer}, device_id_type=MESH)
     own = pltpu.make_async_copy(x_hbm, xin.at[:, HALO : HALO + row_count], local_sem.at[0])
     own.start()
     loads = []
     for k, (src, dst) in enumerate(
-        ((w1_hbm, w1), (w2_hbm, w2), (tk_hbm, tk), (wq_hbm, wq), (wk_hbm, wk), (wv_hbm, wv), (wo_hbm, wo), (w3_hbm, w3))
+        ((w1_hbm, w1), (w2_hbm, w2), (tk_hbm, tk), (wq_hbm, wq), (wk_hbm, wk), (wv_hbm, wv), (wo_hbm, wo), (gain_hbm, gain_ref), (bias_hbm, bias_ref), (w3_hbm, w3))
     ):
         load = pltpu.make_async_copy(src, dst, local_sem.at[k + 1])
         load.start()
         loads.append(load)
 
-    barrier = pltpu.get_barrier_semaphore()
-    above = lax.rem(row + rows_axis - 1, rows_axis)
-    below = lax.rem(row + 1, rows_axis)
-
-    @pl.when(row > 0)
-    def _():
-        pl.semaphore_signal(barrier, inc=1, device_id={"row": above}, device_id_type=MESH)
-
-    @pl.when(row < rows_axis - 1)
-    def _():
-        pl.semaphore_signal(barrier, inc=1, device_id={"row": below}, device_id_type=MESH)
-
-    for k in range(1, frames_axis):
-        peer = lax.rem(frame + k, frames_axis)
-        pl.semaphore_signal(barrier, inc=1, device_id={"frame": peer}, device_id_type=MESH)
     neighbours = (row > 0).astype(jnp.int32) + (row < rows_axis - 1).astype(jnp.int32)
     pl.semaphore_wait(barrier, neighbours + (frames_axis - 1))
 
-    up = pltpu.make_async_remote_copy(
-        src_ref=x_hbm.at[:, 0:HALO],
-        dst_ref=xin.at[:, HALO + row_count : 2 * HALO + row_count],
-        send_sem=halo_send.at[1],
-        recv_sem=halo_recv.at[1],
-        device_id={"row": above},
-        device_id_type=MESH,
-    )
-    down = pltpu.make_async_remote_copy(
-        src_ref=x_hbm.at[:, row_count - HALO : row_count],
-        dst_ref=xin.at[:, 0:HALO],
-        send_sem=halo_send.at[0],
-        recv_sem=halo_recv.at[0],
-        device_id={"row": below},
-        device_id_type=MESH,
-    )
-
-    @pl.when(row > 0)
-    def _():
-        up.start()
-
-    @pl.when(row < rows_axis - 1)
-    def _():
-        down.start()
+    ups, downs = [], []
+    for f in range(local_frames):
+        ups.append(
+            pltpu.make_async_remote_copy(
+                src_ref=x_hbm.at[f, 0:HALO],
+                dst_ref=xin.at[f, HALO + row_count : 2 * HALO + row_count],
+                send_sem=halo_send.at[f, 1],
+                recv_sem=halo_recv.at[f, 1],
+                device_id={"row": above},
+                device_id_type=MESH,
+            )
+        )
+        downs.append(
+            pltpu.make_async_remote_copy(
+                src_ref=x_hbm.at[f, row_count - HALO : row_count],
+                dst_ref=xin.at[f, 0:HALO],
+                send_sem=halo_send.at[f, 0],
+                recv_sem=halo_recv.at[f, 0],
+                device_id={"row": below},
+                device_id_type=MESH,
+            )
+        )
+    for up, down in zip(ups, downs):
+        pl.when(row > 0)(up.start)
+        pl.when(row < rows_axis - 1)(down.start)
 
     blank = jnp.zeros((local_frames, HALO, width, channels), BF16)
 
@@ -166,30 +170,32 @@
     moved[0:1] = edge
     moved[frame_count + 1 : frame_count + 2] = edge
 
-    def spread(first_row, last_row):
-        for f in range(local_frames):
-            rows = xin[f, first_row:last_row]
-            left, right = shifted_columns(rows, width)
-            xs[f, first_row:last_row, :, 0:channels] = left
-            xs[f, first_row:last_row, :, channels : 2 * channels] = rows
-            xs[f, first_row:last_row, :, 2 * channels : 3 * channels] = right
+    def spread(f, first_row, last_row):
+        rows = xin[f, first_row:last_row]
+        left, right = shifted_columns(rows, width)
+        xs[f, first_row:last_row, :, 0:channels] = left
+        xs[f, first_row:last_row, :, channels : 2 * channels] = rows
+        xs[f, first_row:last_row, :, 2 * channels : 3 * channels] = right
 
     own.wait()
-    spread(HALO, HALO + row_count)
+    for f in range(local_frames):
+        spread(f, HALO, HALO + row_count)
     loads[0].wait()
 
-    @pl.when(row > 0)
-    def _():
-        down.wait_recv()
-
-    @pl.when(row < rows_axis - 1)
-    def _():
-        up.wait_recv()
-
-    spread(0, HALO)
-    spread(HALO + row_count, 2 * HALO + row_count)
+    own_part = (local_frames, row_count, width, channels)
+    for i in (0, row_count + 3):
+        partial[:, i] = jnp.zeros((local_frames, width, channels), F32)
+    own_rows = xs[:, HALO : HALO + row_count].reshape(-1, 3 * channels)
+    shares = [
+        matmul(own_rows, w1[a].reshape(3 * channels, channels)).reshape(own_part) for a in range(3)
+    ]
+    for i in range(row_count + 4):
+        terms = [shares[a][:, i + a - HALO] for a in range(3) if 0 <= i + a - HALO < row_count]
+        if terms:
+            partial[:, i] = functools.reduce(jnp.add, terms)
 
     first_rows = row_count + 4
+    exchanges = []
     image_row = (
         lax.broadcasted_iota(jnp.int32, (first_rows, width, channels), 0) + row * row_count - 2
     )
@@ -199,13 +205,20 @@
     )
     second_in = (image_row >= 0) & (image_row < height)
     for f in range(local_frames):
-        summed = None
+        pl.when(row > 0)(downs[f].wait_recv)
+        pl.when(row < rows_axis - 1)(ups[f].wait_recv)
+        spread(f, 0, HALO)
+        spread(f, HALO + row_count, 2 * HALO + row_count)
+        rows = [partial[f, i] for i in range(first_rows)]
         for a in range(3):
+            edges = jnp.concatenate([xs[f, a:HALO], xs[f, HALO + row_count : first_rows + a]], axis=0)
             part = matmul(
-                xs[f, a : a + first_rows].reshape(first_rows * width, 3 * channels),
-                w1[a].reshape(3 * channels, channels),
-            )
-            summed = part if summed is None else summed + part
+                edges.reshape(-1, 3 * channels), w1[a].reshape(3 * channels, channels)
+            ).reshape(-1, width, channels)
+            reached = list(range(HALO - a)) + list(range(HALO + row_count - a, first_rows))
+            for k, i in enumerate(reached):
+                rows[i] = rows[i] + part[k]
+        summed = jnp.concatenate(rows, axis=0)
         first = silu(summed).reshape(first_rows, width, channels)
         first = jnp.where(first_in, first, 0.0).astype(BF16)
         left, right = shifted_columns(first, width)
@@ -213,9 +226,8 @@
         fs[f, :, :, channels : 2 * channels] = first
         fs[f, :, :, 2 * channels : 3 * channels] = right
 
-    loads[1].wait()
-    exchanges = []
-    for f in range(local_frames):
+        if f == 0:
+            loads[1].wait()
         summed = None
         for a in range(3):
             part = matmul(
@@ -240,6 +252,8 @@
             exchanges.append(exchange)
         moved[1 + frame * local_frames + f] = packed[f, frame]
 
+    for load in loads[2:]:
+        load.wait()
     span = frame_count * GROUP
     lane = lax.broadcasted_iota(jnp.int32, (frame_count, span), 1)
     wide = jnp.zeros((frame_count, span), F32)
@@ -260,8 +274,6 @@
     wanted = inner_row * pitch + inner - inner_row * cols + shift
     pick3 = jnp.where(source == wanted, 1.0, 0.0).astype(BF16)
 
-    for load in loads[2:]:
-        load.wait()
     for exchange in exchanges:
         exchange.wait_recv()
 
@@ -312,14 +324,9 @@
         summed = part if summed is None else summed + part
     out_ref[...] = summed.reshape(frame_count, row_count, cols, channels).astype(BF16)
 
-    @pl.when(row > 0)
-    def _():
-        up.wait_send()
-
-    @pl.when(row < rows_axis - 1)
-    def _():
-        down.wait_send()
-
+    for up, down in zip(ups, downs):
+        pl.when(row > 0)(up.wait_send)
+        pl.when(row < rows_axis - 1)(down.wait_send)
     for exchange in exchanges:
         exchange.wait_send()
 
@@ -338,8 +345,8 @@
     square = pltpu.VMEM((channels, channels), BF16)
     return pl.pallas_call(
         functools.partial(kernel, frames_axis, rows_axis),
-        out_shape=jax.ShapeDtypeStruct((frame_count, row_count, cols, channels), BF16),
-        in_specs=[any_space] * 4 + [vmem] + [any_space] * 4 + [vmem, any_space],
+        out_shape=pltpu.VMEM((frame_count, row_count, cols, channels), BF16),
+        in_specs=[any_space] * 11,
         out_specs=vmem,
         scratch_shapes=[
             pltpu.VMEM((local_frames, row_count + 2 * HALO, width, channels), BF16),
@@ -353,14 +360,17 @@
             square,
             square,
             weight,
+            pltpu.VMEM((local_frames, row_count + 4, width, channels), F32),
+            pltpu.VMEM((1, channels), F32),
+            pltpu.VMEM((frame_count, frame_count), F32),
             pltpu.VMEM((frames_axis * slots, (row_count + 2) * width), BF16),
             pltpu.VMEM((local_frames, frames_axis, slots, channels), BF16),
             pltpu.VMEM((frame_count + 2, slots, channels), BF16),
             pltpu.VMEM((frame_count, slots, channels), BF16),
             pltpu.VMEM((3, frame_count, row_count * cols, 3 * channels), BF16),
-            pltpu.SemaphoreType.DMA((9,)),
-            pltpu.SemaphoreType.DMA((2,)),
-            pltpu.SemaphoreType.DMA((2,)),
+            pltpu.SemaphoreType.DMA((11,)),
+            pltpu.SemaphoreType.DMA((local_frames, 2)),
+            pltpu.SemaphoreType.DMA((local_frames, 2)),
             pltpu.SemaphoreType.DMA((local_frames, frames_axis)),
             pltpu.SemaphoreType.DMA((local_frames, frames_axis)),
         ],

time: 18.3 us -> 15.5 us (0.85)
  the two profiles are of different devices: /device:TPU:9 before, /device:TPU:1 now
where the time goes in v2:
time: 15.5 us; the launch traced here: 15.4 us
  Pallas kernels  14.7 us (95%)
  local copies, waits for them, and re-layouts  0.66 us (4%)
    pallas_call x1, Pallas kernels, on_device(): pl.pallas_call(functools.partial(kernel, frames_axis, rows_axis), out_sha...  14.7 us
    unnamed x1, local copies, waits for them, and re-layouts  0.66 us

profile of v2, /device:TPU:1, one launch (start us, length us, event | category | flops | bytes accessed | tf_op | source)
XLA Modules:
  0.0 15.4 jit_solution(15013081253753519284)
XLA Ops:
  0.0 14.7 %shard_map.109 = bf16[8,4,8,256]{3,2,1,0:T(8,128)(2,1)S(1)} custom-call(bf16[2,4,32,256]{3,2,1,0:T(8,128)(2,1)} %x_hbm.1, bf16[3,3,256,256]{3,2,1,0:T(8,128)(2,1)} %w1_hbm.1, bf16[3,3,256,256]{3,2,1,0:T(8,128)(2,1)} %w2_hbm.1, bf16[3,256,256]{2,1,0:T(8,128)(2,1)} %tk_hbm.1, f32[1,256]{1,0:T(1,128)} %bitcast.1, bf16[256,256]{1,0:T(8,128)(2,1)} %wq_hbm.1, ...), custom_call_target="tpu_custom_call" | custom-call | tf_op jit(solution)/shard_map/pallas_call | solution.py:346
  14.7 0.7 %copy.13 = bf16[8,4,8,256]{3,2,1,0:T(8,128)(2,1)} copy(bf16[8,4,8,256]{3,2,1,0:T(8,128)(2,1)S(1)} %shard_map.109) | data formatting | bytes 262144

commit v3 on v2

--- a/solution.py
+++ b/solution.py
@@ -17,6 +17,17 @@
 
 def matmul(lhs, rhs):
     return jnp.dot(lhs, rhs, preferred_element_type=F32)
+
+
+def partner(index, distance, count):
+    if count & (count - 1):
+        return lax.rem(index + distance, count)
+    bit = 1
+    while bit < count:
+        if distance & bit:
+            index = index + bit - 2 * bit * lax.rem(lax.div(index, bit), 2)
+        bit *= 2
+    return index
 
 
 def silu(v):
@@ -123,7 +134,7 @@
     for f in range(local_frames):
         ups.append(
             pltpu.make_async_remote_copy(
-                src_ref=x_hbm.at[f, 0:HALO],
+                src_ref=xin.at[f, HALO : 2 * HALO],
                 dst_ref=xin.at[f, HALO + row_count : 2 * HALO + row_count],
                 send_sem=halo_send.at[f, 1],
                 recv_sem=halo_recv.at[f, 1],
@@ -133,7 +144,7 @@
         )
         downs.append(
             pltpu.make_async_remote_copy(
-                src_ref=x_hbm.at[f, row_count - HALO : row_count],
+                src_ref=xin.at[f, row_count : row_count + HALO],
                 dst_ref=xin.at[f, 0:HALO],
                 send_sem=halo_send.at[f, 0],
                 recv_sem=halo_recv.at[f, 0],
@@ -141,6 +152,7 @@
                 device_id_type=MESH,
             )
         )
+    own.wait()
     for up, down in zip(ups, downs):
         pl.when(row > 0)(up.start)
         pl.when(row < rows_axis - 1)(down.start)
@@ -159,8 +171,13 @@
     source = lax.broadcasted_iota(jnp.int32, (frames_axis * slots, tile_rows * width), 1)
     owner = steps_below(target, slots, frames_axis)
     slot = target - owner * slots
-    slot_row = steps_below(slot, pitch, tile_rows)
-    slot_col = slot - slot_row * pitch + owner * cols - 1
+    inner_slots = tile_rows * cols
+    slot_row = steps_below(slot, cols, tile_rows)
+    slot_col = slot - slot_row * cols
+    side = (slot >= inner_slots + tile_rows).astype(jnp.int32)
+    outer = slot >= inner_slots
+    slot_row = jnp.where(outer, slot - inner_slots - side * tile_rows, slot_row)
+    slot_col = jnp.where(outer, side * (cols + 1) - 1, slot_col) + owner * cols
     wanted = slot_row * width + slot_col
     taken = (
         (slot < tile_rows * pitch) & (slot_col >= 0) & (slot_col < width) & (source == wanted)
@@ -177,7 +194,6 @@
         xs[f, first_row:last_row, :, channels : 2 * channels] = rows
         xs[f, first_row:last_row, :, 2 * channels : 3 * channels] = right
 
-    own.wait()
     for f in range(local_frames):
         spread(f, HALO, HALO + row_count)
     loads[0].wait()
@@ -238,8 +254,8 @@
         second = silu(summed).reshape(tile_rows, width, channels)
         second = jnp.where(second_in, second, 0.0).astype(BF16).reshape(tile_rows * width, channels)
         packed[f] = matmul(pick[...], second).astype(BF16).reshape(frames_axis, slots, channels)
-        for k in range(1, frames_axis):
-            peer = lax.rem(frame + k, frames_axis)
+        for k in reversed(range(1, frames_axis)):
+            peer = partner(frame, k, frames_axis)
             exchange = pltpu.make_async_remote_copy(
                 src_ref=packed.at[f, peer],
                 dst_ref=moved.at[1 + frame * local_frames + f],
@@ -266,12 +282,14 @@
     masked_bias = jnp.where(query_pixel == key_pixel, wide, -1e30)
 
     taps = tile_rows * cols
-    target = lax.broadcasted_iota(jnp.int32, (3 * taps, slots), 0)
-    source = lax.broadcasted_iota(jnp.int32, (3 * taps, slots), 1)
-    shift = steps_below(target, taps, 3)
+    target = lax.broadcasted_iota(jnp.int32, (2 * taps, slots), 0)
+    source = lax.broadcasted_iota(jnp.int32, (2 * taps, slots), 1)
+    shift = (target >= taps).astype(jnp.int32)
     inner = target - shift * taps
     inner_row = steps_below(inner, cols, tile_rows)
-    wanted = inner_row * pitch + inner - inner_row * cols + shift
+    inner_col = inner - inner_row * cols
+    outer = inner_col == shift * (cols - 1)
+    wanted = jnp.where(outer, taps + shift * tile_rows + inner_row, inner + 2 * shift - 1)
     pick3 = jnp.where(source == wanted, 1.0, 0.0).astype(BF16)
 
     for exchange in exchanges:
@@ -285,23 +303,31 @@
     timed = summed.astype(BF16)
     widened = timed.astype(F32)
     scale_inv = lax.rsqrt(jnp.mean(widened * widened, axis=-1, keepdims=True) + 1e-06)
-    normed = (widened * scale_inv * gain_ref[...]).astype(BF16)
+    gained = (widened * gain_ref[...]).astype(BF16)
     tile = (frame_count, slots, channels)
-    queries = matmul(normed, wq[...]).astype(BF16).reshape(tile)
-    key_rows = matmul(normed, wk[...]).astype(BF16).reshape(tile)
-    value_rows = matmul(normed, wv[...]).astype(BF16).reshape(tile)
-    for g in range(slots // GROUP):
-        part = slice(g * GROUP, (g + 1) * GROUP)
-        scores = lax.dot_general(
+    queries = matmul(gained, wq[...])
+    key_rows = matmul(gained, wk[...])
+    value_rows = matmul(gained, wv[...])
+    queries = (queries * scale_inv).astype(BF16).reshape(tile)
+    key_rows = (key_rows * scale_inv).astype(BF16).reshape(tile)
+    value_rows = (value_rows * scale_inv).astype(BF16).reshape(tile)
+    groups = [slice(g * GROUP, (g + 1) * GROUP) for g in range(slots // GROUP)]
+    scores = [
+        lax.dot_general(
             queries[:, part].reshape(span, channels),
             key_rows[:, part].reshape(span, channels),
             (((1,), (1,)), ((), ())),
             preferred_element_type=F32,
         )
-        scores = scores * (1.0 / math.sqrt(channels)) + masked_bias
-        raised = jnp.exp(scores - jnp.max(scores, axis=-1, keepdims=True))
-        probs = (raised / jnp.sum(raised, axis=-1, keepdims=True)).astype(BF16)
-        mixed = matmul(probs, value_rows[:, part].reshape(span, channels))
+        for part in groups
+    ]
+    scores = [score * (1.0 / math.sqrt(channels)) + masked_bias for score in scores]
+    peaks = [jnp.max(score, axis=-1, keepdims=True) for score in scores]
+    raised = [jnp.exp(score - peak) for score, peak in zip(scores, peaks)]
+    totals = [jnp.sum(r, axis=-1, keepdims=True) for r in raised]
+    probs = [(r / total).astype(BF16) for r, total in zip(raised, totals)]
+    for part, prob in zip(groups, probs):
+        mixed = matmul(prob, value_rows[:, part].reshape(span, channels))
         context[:, part] = mixed.astype(BF16).reshape(frame_count, GROUP, channels)
     attended = widened + matmul(context[...].reshape(pixels, channels), wo[...])
     attended = attended.astype(BF16).reshape(tile)
@@ -309,11 +335,12 @@
     count = row_count * cols
     for f in range(frame_count):
         gathered = matmul(pick3, attended[f])
+        middle = attended[f, 0:taps].astype(F32)
+        columns = (gathered[0:taps], middle, gathered[taps : 2 * taps])
         for a in range(3):
             for b in range(3):
-                start = b * taps + a * cols
-                cols3[a, f, :, b * channels : (b + 1) * channels] = gathered[
-                    start : start + count
+                cols3[a, f, :, b * channels : (b + 1) * channels] = columns[b][
+                    a * cols : a * cols + count
                 ].astype(BF16)
     summed = None
     for a in range(3):

time: 15.5 us -> 15.1 us (0.974)
  Pallas kernels: 14.7 us -> 14.3 us
    pallas_call x1, Pallas kernels: 14.7 us -> 14.3 us  [on_device(): pl.pallas_call(functools.partial(kernel, frames_axis, rows_axis), out_sha...]
where the time goes in v3:
time: 15.1 us; the launch traced here: 14.9 us
  Pallas kernels  14.3 us (95%)
  local copies, waits for them, and re-layouts  0.66 us (4%)
    pallas_call x1, Pallas kernels, on_device(): pl.pallas_call(functools.partial(kernel, frames_axis, rows_axis), out_sha...  14.3 us
    unnamed x1, local copies, waits for them, and re-layouts  0.66 us

profile of v3, /device:TPU:1, one launch (start us, length us, event | category | flops | bytes accessed | tf_op | source)
XLA Modules:
  0.0 14.9 jit_solution(6026788983267641915)
XLA Ops:
  0.0 14.3 %shard_map.109 = bf16[8,4,8,256]{3,2,1,0:T(8,128)(2,1)S(1)} custom-call(bf16[2,4,32,256]{3,2,1,0:T(8,128)(2,1)} %x_hbm.1, bf16[3,3,256,256]{3,2,1,0:T(8,128)(2,1)} %w1_hbm.1, bf16[3,3,256,256]{3,2,1,0:T(8,128)(2,1)} %w2_hbm.1, bf16[3,256,256]{2,1,0:T(8,128)(2,1)} %tk_hbm.1, f32[1,256]{1,0:T(1,128)} %bitcast.1, bf16[256,256]{1,0:T(8,128)(2,1)} %wq_hbm.1, ...), custom_call_target="tpu_custom_call" | custom-call | tf_op jit(solution)/shard_map/pallas_call | solution.py:373
  14.3 0.7 %copy.13 = bf16[8,4,8,256]{3,2,1,0:T(8,128)(2,1)} copy(bf16[8,4,8,256]{3,2,1,0:T(8,128)(2,1)S(1)} %shard_map.109) | data formatting | bytes 262144
